TPU v7x, 256 devices: a whole 4x4x8 slice. The times are simulated.
256 devices in a mesh: tm: 64 (over x, z, core), rows: 4 (over y).
Axes of the slice: x: 4, y: 4, z: 8, core: 2. Of those that a mesh axis runs over, the one named last changes fastest.
Arguments:
- features: bfloat16 [128, 4, 160, 512], P('tm', 'rows'), may hold values from -25 to 25
- norm_gain: float32 [512], replicated, may hold values from 0.1 to 1.9
- norm_bias: float32 [512], replicated, may hold values from -1 to 1
- weight: bfloat16 [3, 3, 3, 512, 256], replicated, may hold values from -0.0546875 to 0.0546875
- upstream: bfloat16 [128, 4, 160, 256], P('tm', 'rows'), may hold values from -20 to 20
Outputs:
- grad_features: bfloat16 [128, 4, 160, 512], P('tm', 'rows')
- grad_weight: float32 [3, 3, 3, 512, 256], P(None, None, None, 'tm', 'rows')
- grad_gain: float32 [512], replicated
- grad_bias: float32 [512], replicated
All inputs are finite; a program needn't handle non-finite values.
Results may differ from a plain program's by a relative error of at most 0.0015.
Values may be sent and summed in bfloat16 or wider, within the bound.
No kernel may reach another device: no remote copies, remote signals or barrier semaphores. Data moves between devices by JAX's collectives and lax.ppermute only.
A program may use at most 64 MiB of HBM per device.

v0:
```python
import functools

import jax
import jax.numpy as jnp
from jax import lax
from jax.experimental import pallas as pl
from jax.experimental.pallas import tpu as pltpu
from jax.sharding import PartitionSpec as P


GROUPS = 32
EPS = 1e-06
TEAM = 4
SHARES = ((0, 192), (192, 384), (384, 576), (576, 800))
HALF = 112
EDGES = ((1, 0), (0, -1), (0, 1), (1, -1), (1, 1))
F32 = jnp.float32
BF16 = jnp.bfloat16


def iota(shape, dim):
    return lax.broadcasted_iota(jnp.int32, shape, dim)


def shift_of(value):
    return value.bit_length() - 1


def exact_dot(a, ones, dims=((1,), (0,))):
    high = a.astype(BF16).astype(F32)
    rest = a - high
    mid = rest.astype(BF16).astype(F32)
    parts = jnp.concatenate([high, mid, rest - mid, jnp.zeros_like(a)], axis=0).astype(BF16)
    out = lax.dot_general(parts, ones, (dims, ((), ())), preferred_element_type=F32)
    return out[0:8] + out[8:16] + out[16:24]


def ones_where(mask):
    return jnp.where(mask, 1.0, 0.0).astype(BF16)


def members(chans, offset):
    bits = shift_of(chans // GROUPS)
    return ones_where(lax.shift_right_logical(iota((chans, 128), 0), bits) == iota((chans, 128), 1) - offset)


def sources(lane, chans, teams, spot):
    step = chans // teams
    return (lane & -step) * TEAM + spot * step + (lane & (step - 1))


def sigmoid(value):
    return 0.5 * jnp.tanh(0.5 * value) + 0.5


def col_shifts(slab):
    cols = slab.shape[0]
    wide = slab.astype(F32)
    row = iota(wide.shape, 0)
    ahead = jnp.where(row < cols - 1, pltpu.roll(wide, cols - 1, 0), 0.0).astype(BF16)
    behind = jnp.where(row > 0, pltpu.roll(wide, 1, 0), 0.0).astype(BF16)
    return ahead, slab, behind


def pack_kernel(teams, feats_ref, up_ref, later_ref, load_ref):
    positions, chans = feats_ref.shape
    cols = up_ref.shape[1]
    rows = load_ref.shape[1]
    feats = feats_ref[...]
    wide = chans // TEAM
    lane = iota((1, chans), 1)
    source = sources(lane & (wide - 1), chans, teams, lax.shift_right_logical(lane, shift_of(wide)))
    mover = ones_where(iota((chans, chans), 0) == source)
    moved = jnp.dot(feats, mover, preferred_element_type=F32).astype(BF16)
    outs = up_ref.shape[2] // rows
    for j in range(TEAM):
        for r in range(rows):
            load_ref[j, r, 0:positions, :] = moved[:, j * wide : (j + 1) * wide]
    order = lax.axis_index("tm") & (TEAM - 1)
    for r in range(rows):
        own, after = (
            jnp.concatenate(
                [ref[0, :, r * outs : (r + 1) * outs], ref[1, :, r * outs : (r + 1) * outs]], axis=1
            )
            for ref in (up_ref, later_ref)
        )
        for d in range(TEAM):

            @pl.when(order == d)
            def _():
                first, last = (value - d * cols for value in SHARES[d])
                share = jnp.concatenate([own[first:], after[0 : last - cols]], axis=0)
                size = (last - first) // 2
                for j in range(TEAM):
                    core = j % 2
                    part = share[core * size : (core + 1) * size]
                    load_ref[j, r, positions : positions + size, :] = part


def stats_kernel(feats_ref, out_ref):
    positions, chans = feats_ref.shape
    floats = feats_ref[...].astype(F32)
    first = members(chans, 0)
    second = members(chans, GROUPS)
    total = jnp.broadcast_to(jnp.sum(floats, axis=0, keepdims=True), (8, chans))
    mean = exact_dot(total, first) / (positions * (chans // GROUPS))
    diffs = floats - exact_dot(mean, first, ((1,), (1,)))[0:1]
    squares = jnp.broadcast_to(jnp.sum(diffs * diffs, axis=0, keepdims=True), (8, chans))
    out_ref[...] = jnp.broadcast_to((mean + exact_dot(squares, second))[None], out_ref.shape)


def combine_kernel(count, load_ref, stats_ref, out_ref, parts, sem):
    stats = [stats_ref[g] for g in range(stats_ref.shape[0])]
    total = stats[0]
    for stat in stats[1:]:
        total = total + stat
    mean = total / len(stats)
    spans = jnp.zeros_like(mean)
    for stat in stats:
        spans = spans + (stat - mean) * (stat - mean)
    lane = iota((8, 128), 1)
    stat = jnp.where(lane < GROUPS, mean, total + count * pltpu.roll(spans, GROUPS, 1))
    high = stat.astype(BF16).astype(F32)
    mid = (stat - high).astype(BF16).astype(F32)
    low = stat - high - mid
    row = iota((8, 128), 0)
    rows = jnp.where(row == 0, high, jnp.where(row == 1, mid, jnp.where(row == 2, low, 0.0)))
    rows = jnp.concatenate([rows, jnp.zeros_like(rows)], axis=0).astype(BF16)
    parts[...] = jnp.broadcast_to(rows[None], parts.shape)
    copy = pltpu.make_async_copy(parts, out_ref.at[:, pl.ds(out_ref.shape[1] - 16, 16)], sem)
    copy.start()
    copy.wait()


def dense_kernel(
    up_ref, above_ref, below_ref, later_ref, later_above_ref, later_below_ref, weight_ref, out_ref, slabs
):
    step = pl.program_id(0)
    time_tap = step // 3
    row_tap = step % 3
    time_index = lax.axis_index("tm")
    row_index = lax.axis_index("rows")
    positions = out_ref.shape[0]
    cols = up_ref.shape[1]

    @pl.when(step == 0)
    def _():
        out_ref[...] = jnp.zeros_like(out_ref)
        more = (time_index < lax.axis_size("tm") - 1).astype(F32)
        up_ok = (row_index > 0).astype(F32)
        down_ok = (row_index < lax.axis_size("rows") - 1).astype(F32)
        for f in range(4):
            trio = (above_ref, up_ref, below_ref) if f < 2 else (later_above_ref, later_ref, later_below_ref)
            tail = jnp.float32(1.0) if f < 2 else more
            for r, keep in enumerate((up_ok, jnp.float32(1.0), down_ok)):
                slab = (trio[r][f % 2].astype(F32) * (keep * tail)).astype(BF16)
                for c, moved in enumerate(col_shifts(slab)):
                    slabs[c, r, f] = moved

    def product(slab, c):
        return lax.dot_general(
            slab, weight_ref[0, 0, c], (((1,), (1,)), ((), ())), preferred_element_type=F32
        )

    total = out_ref[...]
    for c in range(3):
        slab = slabs[c, 2 - row_tap, pl.ds(2 - time_tap, 2)].reshape(positions, -1)
        total = total + product(slab, c)
    out_ref[...] = total

    @pl.when(jnp.logical_and(time_index == 0, time_tap == 0))
    def _():
        for c in range(3):
            both = slabs[c, 2 - row_tap, pl.ds(0, 2)].reshape(positions, -1)
            both = product(both, c)
            out_ref[0:cols, :] += both[0:cols] + both[cols:]

    @pl.when(jnp.logical_and(time_index == 0, time_tap == 1))
    def _():
        for c in range(3):
            out_ref[0:cols, :] += product(slabs[c, 2 - row_tap, 0], c)


def norm_rows(stats, chans, positions):
    devices = stats.shape[0]
    size = chans // GROUPS
    first = members(chans, 0)
    second = members(chans, GROUPS)
    total = jnp.sum(stats, axis=0, keepdims=True)
    centre = total / devices
    spans = stats - centre
    spans = jnp.sum(spans * spans, axis=0, keepdims=True)
    dims = ((1,), (1,))
    parts = exact_dot(jnp.broadcast_to(total, (8, 128)), second, dims) / (devices * positions * size)
    parts = parts + exact_dot(jnp.broadcast_to(spans, (8, 128)), first, dims) / devices
    inverse = lax.rsqrt(parts + EPS)
    centre = exact_dot(jnp.broadcast_to(centre, (8, 128)), first, dims)
    return centre, inverse


def act_kernel(
    positions, feats_ref, gain_ref, bias_ref, load_ref, dense_ref, act_ref, sums_ref, norm_ref, swap_ref
):
    chans = gain_ref.shape[1]
    start = load_ref.shape[2] - 16
    stats = []
    for j in range(load_ref.shape[0]):
        for r in range(load_ref.shape[1]):
            parts = load_ref[j, r, start:].astype(F32)
            stats.append(parts[0:1] + parts[1:2] + parts[2:3])
    swap_ref[...] = load_ref[:, :, start - HALF : start, :]
    centre, inverse = norm_rows(jnp.concatenate(stats, axis=0), chans, positions)
    norm_ref[0:8] = centre
    norm_ref[8:16] = inverse
    centre = centre[0:1]
    inverse = inverse[0:1]
    normed = (feats_ref[...].astype(F32) - centre) * inverse
    preact = normed * gain_ref[...] + bias_ref[...]
    sig = sigmoid(preact)
    act = dense_ref[...] * sig * (1.0 + preact * (1.0 - sig))
    act_ref[...] = act
    gains = jnp.sum(act * normed, axis=0, keepdims=True)
    biases = jnp.sum(act, axis=0, keepdims=True)
    pieces = chans // 128
    rows = [gains[:, p * 128 : (p + 1) * 128] for p in range(pieces)]
    rows = rows + [biases[:, p * 128 : (p + 1) * 128] for p in range(pieces)]
    sums_ref[...] = jnp.broadcast_to(jnp.concatenate(rows, axis=0)[None], sums_ref.shape)


def append_kernel(part_ref, load_ref, out_ref):
    total = load_ref[0]
    for g in range(1, load_ref.shape[0]):
        total = total + load_ref[g]
    place = (out_ref.shape[0],) + total.shape
    out_ref[:, out_ref.shape[1] - total.shape[0] :, :] = jnp.broadcast_to(total[None], place)


def weight_kernel(teams, load_ref, other_ref, norm_ref, gain_ref, bias_ref, out_ref, hidden, acc):
    time_index = lax.axis_index("tm")
    rows = load_ref.shape[1]
    cols = hidden.shape[2]
    chans = gain_ref.shape[1]
    wide = chans // TEAM
    step = chans // teams
    mover = ones_where(
        iota((chans, wide), 0) == sources(iota((1, wide), 1), chans, teams, time_index & (TEAM - 1))
    )

    def slice_of(value):
        return exact_dot(value, mover)[0:1]

    centre = slice_of(norm_ref[0:8])
    inverse = slice_of(norm_ref[8:16])
    gain = slice_of(jnp.broadcast_to(gain_ref[...], (8, chans)))
    bias = slice_of(jnp.broadcast_to(bias_ref[...], (8, chans)))

    def silu(value):
        preact = (value.astype(F32) - centre) * inverse * gain + bias
        return (preact * sigmoid(preact)).astype(BF16)

    frames = 2 * TEAM
    for f in range(frames + 2):
        hidden[f, 0] = jnp.zeros(hidden.shape[2:], BF16)
        hidden[f, rows + 1] = jnp.zeros(hidden.shape[2:], BF16)
    opening = (time_index < TEAM).astype(F32)
    for j in range(TEAM):
        for r in range(rows):
            for f in range(2):
                value = silu(load_ref[j, r, f * cols : (f + 1) * cols, :])
                hidden[2 + 2 * j + f, 1 + r] = value
                if j == 0 and f == 0:
                    value = (value.astype(F32) * opening).astype(BF16)
                    hidden[0, 1 + r] = value
                    hidden[1, 1 + r] = value

    base = 2 * cols

    def pieces_of(q, r):
        pieces = []
        for d, (begin, close) in enumerate(SHARES):
            size = (close - begin) // 2
            for half in range(2):
                first = max(q * cols, begin + half * size) - begin - half * size
                last = min((q + 1) * cols, begin + (half + 1) * size) - begin - half * size
                if first < last:
                    mine = load_ref[d, r, base + first : base + last, :]
                    pieces.append(jnp.where((time_index & 1) == half, mine, other_ref[d, r, first:last, :]))
        return pieces

    lanes = iota((cols, 128), 1) < 64
    more = (time_index < lax.axis_size("tm") - TEAM).astype(F32)
    for j in range(TEAM + 1):
        halves = [[], []]
        for r in range(rows):
            pair = jnp.concatenate(pieces_of(j, r), axis=0).astype(F32)
            if j == TEAM:
                pair = pair * more
            row = iota(pair.shape, 0)
            ahead = jnp.where(row < cols - 1, pltpu.roll(pair, cols - 1, 0), 0.0)
            behind = jnp.where(row > 0, pltpu.roll(pair, 1, 0), 0.0)
            left = jnp.where(lanes, ahead, pltpu.roll(pair, 64, 1))
            right = jnp.where(lanes, pltpu.roll(ahead, 64, 1), pair)
            halves[0].append(jnp.concatenate([left, behind[:, 0:64]], axis=1))
            halves[1].append(jnp.concatenate([right, behind[:, 64:128]], axis=1))

        def taps_of(frame, depth):
            taps = [
                hidden[frame + a, b : b + rows].reshape(rows * cols, wide) for a in range(depth) for b in range(3)
            ]
            return jnp.concatenate(taps, axis=1)

        sides = [jnp.concatenate(halves[f], axis=0).astype(BF16) for f in range(2)]
        if j < TEAM:
            jobs = [(jnp.concatenate(sides, axis=0), [taps_of(2 * j + f, 3) for f in range(2)], 3)]
        else:
            jobs = [(sides[f], [taps_of(2 * j + f, 2 - f)], 2 - f) for f in range(2)]
        for side, taps, depth in jobs:
            term = lax.dot_general(
                side, jnp.concatenate(taps, axis=0), (((0,), (0,)), ((), ())), preferred_element_type=F32
            )
            if j == 0:
                acc[...] = term
            else:
                acc[:, 0 : 3 * depth * wide] += term

    groups = out_ref.shape[0]
    tail = None
    for ab in range(9):
        block = acc[:, ab * wide : (ab + 1) * wide].T
        out_ref[:, ab * step : (ab + 1) * step, :] = block[:, 0:128].reshape(groups, step, 128)
        last = block[:, 128:192]
        if ab % 2 == 0:
            tail = last
        if ab % 2 == 1 or ab == 8:
            both = jnp.concatenate([tail, last], axis=1)
            at = (9 + ab // 2) * step
            out_ref[:, at : at + step, :] = both.reshape(groups, step, 128)


def final_kernel(
    count, load_ref, act_ref, feats_ref, norm_ref, gain_ref, out_ref, grad_ref, gain_out_ref, bias_out_ref
):
    chans = gain_ref.shape[1]
    pieces = chans // 128
    step = grad_ref.shape[2]
    total = load_ref[0]
    for g in range(1, load_ref.shape[0]):
        total = total + load_ref[g]
    for ab in range(9):
        part = total[ab * step : (ab + 1) * step]
        grad_ref[ab, 0] = part[:, 0:64]
        grad_ref[ab, 1] = part[:, 64:128]
        at = (9 + ab // 2) * step
        side = 64 * (ab % 2)
        grad_ref[ab, 2] = total[at : at + step, side : side + 64]
    total = total[14 * step :]
    gains = jnp.concatenate([total[p : p + 1] for p in range(pieces)], axis=1)
    biases = jnp.concatenate([total[pieces + p : pieces + p + 1] for p in range(pieces)], axis=1)
    gain_out_ref[...] = gains
    bias_out_ref[...] = biases
    gain = gain_ref[...]
    owner = members(chans, 0)

    def spread(value):
        value = exact_dot(jnp.broadcast_to(value, (8, chans)), owner) / count
        return exact_dot(value, owner, ((1,), (1,)))[0:1]

    first = spread(gain * biases)
    second = spread(gain * gains)
    centre = norm_ref[0:1]
    inverse = norm_ref[8:9]
    normed = (feats_ref[...].astype(F32) - centre) * inverse
    out_ref[...] = (inverse * (act_ref[...] * gain - first - normed * second)).astype(BF16)


def on_device(features, norm_gain, norm_bias, weight, upstream):
    frames, rows_dev, cols, chans = features.shape
    outs = upstream.shape[3]
    tms = lax.axis_size("tm")
    rows = lax.axis_size("rows")
    devices = tms * rows
    positions = frames * rows_dev * cols
    step = chans // tms
    groups = tms // TEAM
    wide = chans // TEAM
    count = positions * devices * (chans // GROUPS)
    vmem = pl.BlockSpec(memory_space=pltpu.VMEM)
    far = pl.BlockSpec(memory_space=pltpu.HBM)

    def params(mebibytes):
        return pltpu.CompilerParams(vmem_limit_bytes=mebibytes * 1024 * 1024)

    feats = features.reshape(positions, chans)
    ups = upstream.reshape(frames, cols, outs)
    gain = norm_gain.reshape(1, chans)
    bias = norm_bias.reshape(1, chans)
    size = TEAM * rows
    length = positions + HALF + 16
    teams = [[size * g + i for i in range(size)] for g in range(groups)]
    ranks = [[TEAM * g + j for g in range(groups)] for j in range(TEAM)]

    def in_teams(value):
        return lax.all_to_all(value, ("tm", "rows"), 0, 0, tiled=True, axis_index_groups=teams)

    def in_ranks(value):
        return lax.all_to_all(value, "tm", 0, 0, tiled=True, axis_index_groups=ranks)

    def neighbour(tm_step, row_step):
        pairs = [
            (((t + tm_step) % tms) * rows + (r + row_step) % rows, t * rows + r)
            for t in range(tms)
            for r in range(rows)
        ]
        return lax.ppermute(ups, ("tm", "rows"), pairs)

    halos = [neighbour(a, b) for a, b in EDGES]

    stats = pl.pallas_call(
        stats_kernel,
        out_shape=jax.ShapeDtypeStruct((groups, 8, 128), F32),
        compiler_params=params(62),
        name="stats",
    )(feats)
    stats = in_ranks(stats)
    pack_call = pl.pallas_call(
        functools.partial(pack_kernel, tms),
        out_shape=jax.ShapeDtypeStruct((TEAM, rows, length, wide), BF16),
        compiler_params=params(62),
        name="pack",
    )
    load = pack_call(feats, ups, halos[0])
    load = pl.pallas_call(
        functools.partial(combine_kernel, float(positions * (chans // GROUPS))),
        in_specs=[far, vmem],
        out_specs=far,
        out_shape=jax.ShapeDtypeStruct((size, length, wide), BF16),
        scratch_shapes=[pltpu.VMEM((size, 16, wide), BF16), pltpu.SemaphoreType.DMA],
        input_output_aliases={0: 0},
        compiler_params=params(61),
        name="combine",
    )(load.reshape(size, length, wide), stats)
    load = in_teams(load).reshape(TEAM, rows, length, wide)

    def whole(shape):
        return pl.BlockSpec(shape, lambda *s: (0,) * len(shape))

    dense_call = pl.pallas_call(
        dense_kernel,
        grid=(9,),
        in_specs=[
            *[whole((frames, cols, outs))] * 6,
            pl.BlockSpec((1, 1, 3, chans, outs), lambda s: (s // 3, s % 3, 0, 0, 0)),
        ],
        out_specs=whole((positions, chans)),
        out_shape=jax.ShapeDtypeStruct((positions, chans), F32),
        scratch_shapes=[pltpu.VMEM((3, 3, 4, cols, outs), BF16)],
        compiler_params=params(62),
        name="dense",
    )
    dense = dense_call(ups, halos[1], halos[2], halos[0], halos[3], halos[4], weight)

    act, sums, norm, swap = pl.pallas_call(
        functools.partial(act_kernel, positions * groups),
        in_specs=[pl.BlockSpec()] * 3 + [vmem, pl.BlockSpec()],
        out_shape=(
            jax.ShapeDtypeStruct((positions, chans), F32),
            jax.ShapeDtypeStruct((size, 8, 128), F32),
            jax.ShapeDtypeStruct((16, chans), F32),
            jax.ShapeDtypeStruct((TEAM, rows, HALF, wide), BF16),
        ),
        compiler_params=params(60),
        name="act",
    )(feats, gain, bias, load, dense)
    other = lax.ppermute(swap, "tm", [(t, t ^ 1) for t in range(tms)])
    sums = in_teams(sums)

    weight_call = pl.pallas_call(
        functools.partial(weight_kernel, tms),
        in_specs=[vmem] + [pl.BlockSpec()] * 4,
        out_specs=vmem,
        out_shape=jax.ShapeDtypeStruct((groups, 14 * step + 8, 128), F32),
        scratch_shapes=[
            pltpu.VMEM((2 * TEAM + 2, rows + 2, cols, wide), BF16),
            pltpu.VMEM((3 * 64, 9 * wide), F32),
        ],
        compiler_params=params(52),
        name="wgrad",
    )
    part = weight_call(load, other, norm, gain, bias)
    part = pl.pallas_call(
        append_kernel,
        in_specs=[vmem, vmem],
        out_specs=vmem,
        out_shape=jax.ShapeDtypeStruct((groups, 14 * step + 8, 128), F32),
        input_output_aliases={0: 0},
        compiler_params=params(16),
        name="append",
    )(part, sums)
    part = in_ranks(part)

    grad_features, grad_weight, grad_gain, grad_bias = pl.pallas_call(
        functools.partial(final_kernel, count),
        in_specs=[vmem] + [pl.BlockSpec()] * 4,
        out_shape=(
            jax.ShapeDtypeStruct((positions, chans), BF16),
            jax.ShapeDtypeStruct((9, 3, step, outs // rows), F32),
            jax.ShapeDtypeStruct((1, chans), F32),
            jax.ShapeDtypeStruct((1, chans), F32),
        ),
        compiler_params=params(16),
        name="final",
    )(part, act, feats, norm, gain)
    return (
        grad_features.reshape(features.shape),
        grad_weight.reshape(3, 3, 3, step, outs // rows),
        grad_gain.reshape(chans),
        grad_bias.reshape(chans),
    )


def solution(mesh):
    in_specs = (P("tm", "rows", None, None), P(), P(), P(), P("tm", "rows", None, None))
    out_specs = (P("tm", "rows", None, None), P(None, None, None, "tm", "rows"), P(), P())
    return jax.shard_map(on_device, mesh=mesh, in_specs=in_specs, out_specs=out_specs, check_vma=False)
```

profile of v0, /device:TPU:32, one launch (start us, length us, event | category | flops | bytes accessed | tf_op | source)
XLA Modules:
  0.0 121.4 jit_solution(2179880535859214870)
XLA Ops:
  0.6 0.1 collective-permute-start
  0.7 2.2 %stats.1 = f32[16,8,128]{2,1,0:T(8,128)} custom-call(bf16[320,512]{1,0:T(8,128)(2,1)} %bitcast.12), custom_call_target="tpu_custom_call" | custom-call | tf_op jit(solution)/shard_map/stats/pallas_call | solution.py:418
  2.9 10.6 %all-to-all-start = ((f32[16,8,128]{2,1,0:T(8,128)}), f32[16,8,128]{2,1,0:T(8,128)S(1)}, u32[]{:S(2)}, u32[]{:S(2)}) async-start(f32[16,8,128]{2,1,0:T(8,128)} %stats.1), calls=%async_computation | async-start | bytes 131072 | tf_op jit(solution)/shard_map/all_to_all | solution.py:406
  13.5 0.7 copy-done.7
  14.2 3.0 %pack.1 = bf16[4,4,448,128]{3,2,1,0:T(8,128)(2,1)} custom-call(bf16[320,512]{1,0:T(8,128)(2,1)} %bitcast.13, bf16[2,160,256]{2,1,0:T(8,128)(2,1)} %bitcast.23, bf16[2,160,256]{2,1,0:T(8,128)(2,1)} %copy-done.7), custom_call_target="tpu_custom_call" | custom-call | tf_op jit(solution)/shard_map/pack/pallas_call | solution.py:431
  17.2 6.5 %all-to-all-done.stats_ref = f32[16,8,128]{2,1,0:T(8,128)S(1)} async-done(((f32[16,8,128]{2,1,0:T(8,128)}), f32[16,8,128]{2,1,0:T(8,128)S(1)}, u32[]{:S(2)}, u32[]{:S(2)}) %all-to-all-start) | async-done | bytes 65568 | tf_op jit(solution)/shard_map/all_to_all | solution.py:406
  23.7 0.6 copy-done.8
  24.3 1.6 %combine.1 = bf16[16,448,128]{2,1,0:T(8,128)(2,1)} custom-call(bf16[16,448,128]{2,1,0:T(8,128)(2,1)} %bitcast.21, f32[16,8,128]{2,1,0:T(8,128)} %copy-done.8), custom_call_target="tpu_custom_call", output_to_operand_aliasing={{}: (0, {})} | custom-call | tf_op jit(solution)/shard_map/combine/pallas_call | solution.py:432
  26.0 6.1 %all-to-all-start.1 = ((bf16[16,448,128]{2,1,0:T(8,128)(2,1)}), bf16[16,448,128]{2,1,0:T(8,128)(2,1)}, u32[]{:S(2)}, u32[]{:S(2)}) async-start(bf16[16,448,128]{2,1,0:T(8,128)(2,1)} %combine.1), calls=%async_computation.1 | async-start | bytes 3670016 | tf_op jit(solution)/shard_map/all_to_all | solution.py:403
  32.1 1.5 %collective-permute-start.1 = (bf16[2,160,256]{2,1,0:T(8,128)(2,1)S(1)}, bf16[2,160,256]{2,1,0:T(8,128)(2,1)S(1)}, u32[]{:S(2)}, u32[]{:S(2)}) collective-permute-start(bf16[2,160,256]{2,1,0:T(8,128)(2,1)S(1)} %bitcast.25), channel_id=1, source_target_pairs={{3,0},{0,1},{1,2},{2,3},{7,4},{4,5},{5,6},{6,7},{11,8},{8,9},{9,10... | collective-permute-start | bytes 491528 | tf_op jit(solution)/shard_map/ppermute | solution.py:414
  33.6 1.8 %collective-permute-start.2 = (bf16[2,160,256]{2,1,0:T(8,128)(2,1)S(1)}, bf16[2,160,256]{2,1,0:T(8,128)(2,1)S(1)}, u32[]{:S(2)}, u32[]{:S(2)}) collective-permute-start(bf16[2,160,256]{2,1,0:T(8,128)(2,1)S(1)} %bitcast.26), channel_id=1, source_target_pairs={{1,0},{2,1},{3,2},{0,3},{5,4},{6,5},{7,6},{4,7},{9,8},{10,9},{11,1... | collective-permute-start | bytes 491528 | tf_op jit(solution)/shard_map/ppermute | solution.py:414
  35.4 2.5 %collective-permute-start.4 = (bf16[2,160,256]{2,1,0:T(8,128)(2,1)S(1)}, bf16[2,160,256]{2,1,0:T(8,128)(2,1)S(1)}, u32[]{:S(2)}, u32[]{:S(2)}) collective-permute-start(bf16[2,160,256]{2,1,0:T(8,128)(2,1)S(1)} %bitcast.28), channel_id=1, source_target_pairs={{5,0},{6,1},{7,2},{4,3},{9,4},{10,5},{11,6},{8,7},{13,8},{14,9},{1... | collective-permute-start | bytes 491528 | tf_op jit(solution)/shard_map/ppermute | solution.py:414
  37.9 23.3 %collective-permute-done.1.above_ref = bf16[2,160,256]{2,1,0:T(8,128)(2,1)S(1)} collective-permute-done((bf16[2,160,256]{2,1,0:T(8,128)(2,1)S(1)}, bf16[2,160,256]{2,1,0:T(8,128)(2,1)S(1)}, u32[]{:S(2)}, u32[]{:S(2)}) %collective-permute-start.1) | collective-permute-done | bytes 163872 | tf_op jit(solution)/shard_map/ppermute | solution.py:414
  61.2 1.4 %collective-permute-done.3.later_above_ref = bf16[2,160,256]{2,1,0:T(8,128)(2,1)S(1)} collective-permute-done((bf16[2,160,256]{2,1,0:T(8,128)(2,1)S(1)}, bf16[2,160,256]{2,1,0:T(8,128)(2,1)S(1)}, u32[]{:S(2)}, u32[]{:S(2)}) %collective-permute-start.3) | collective-permute-done | bytes 163872 | tf_op jit(solution)/shard_map/ppermute | solution.py:414
  62.6 0.7 copy-done.11
  63.3 0.7 copy-done.12
  63.9 9.8 %dense.1.dense_ref = f32[320,512]{1,0:T(8,128)} custom-call(bf16[2,160,256]{2,1,0:T(8,128)(2,1)} %bitcast.24, bf16[2,160,256]{2,1,0:T(8,128)(2,1)} %copy-done.9, bf16[2,160,256]{2,1,0:T(8,128)(2,1)} %copy-done.10, bf16[2,160,256]{2,1,0:T(8,128)(2,1)} %copy-done.7, bf16[2,160,256]{2,1,0:T(8,128)(2,1)} %copy-done.11, bf16[2,160,256]{2,1,0:T(8,128)(2,1)} %copy-done.12, ...), custom_call_target="tpu_custom_call" | custom-call | tf_op jit(solution)/shard_map/dense/pallas_call | solution.py:460
  73.7 3.6 %act.1 = (f32[320,512]{1,0:T(8,128)}, f32[16,8,128]{2,1,0:T(8,128)}, f32[16,512]{1,0:T(8,128)}, bf16[4,4,112,128]{3,2,1,0:T(8,128)(2,1)}) custom-call(bf16[320,512]{1,0:T(8,128)(2,1)} %bitcast.14, f32[1,512]{1,0:T(1,128)} %bitcast.16, f32[1,512]{1,0:T(1,128)} %bitcast.19, bf16[4,4,448,128]{3,2,1,0:T(8,128)(2,1)} %bitcast.3.load_ref, f32[320,512]{1,0:T(8,128)} %dense.1.dense_ref), custom_call_target="tpu_custom_call" | custom-call | tf_op jit(solution)/shard_map/act/pallas_call | solution.py:462
  77.3 5.2 %all-to-all-start.2 = ((f32[16,8,128]{2,1,0:T(8,128)}), f32[16,8,128]{2,1,0:T(8,128)S(1)}, u32[]{:S(2)}, u32[]{:S(2)}) async-start(f32[16,8,128]{2,1,0:T(8,128)} %get-tuple-element.14), calls=%async_computation.2 | async-start | bytes 131072 | tf_op jit(solution)/shard_map/all_to_all | solution.py:403
  82.5 0.0 copy-start.2
  82.5 0.7 copy-done.2
  83.3 5.4 %wgrad.1.part_ref = f32[16,120,128]{2,1,0:T(8,128)S(1)} custom-call(bf16[4,4,448,128]{3,2,1,0:T(8,128)(2,1)} %bitcast.3.load_ref, bf16[4,4,112,128]{3,2,1,0:T(8,128)(2,1)S(1)} %collective-permute-done.5.other_ref, f32[16,512]{1,0:T(8,128)S(1)} %copy-done.2, f32[1,512]{1,0:T(1,128)S(1)} %bitcast.17, f32[1,512]{1,0:T(1,128)S(1)} %bitcast.20), custom_call_target="tpu_custom_call" | custom-call | tf_op jit(solution)/shard_map/wgrad/pallas_call | solution.py:489
  88.8 31.2 %all_to_all.20.load_ref = f32[16,120,128]{2,1,0:T(8,128)S(1)} all-to-all(f32[16,120,128]{2,1,0:T(8,128)S(1)} %append.1), channel_id=1, replica_groups={{0,16,32,48,64,80,96,112,128,144,160,176,192,208,224,240},{4,20,36,52,6..., dimensions={0} | all-to-all | bytes 1966080 | tf_op jit(solution)/shard_map/all_to_all | solution.py:406
  120.0 1.4 %final.1 = (bf16[320,512]{1,0:T(8,128)(2,1)}, f32[9,3,8,64]{3,2,1,0:T(8,128)}, f32[1,512]{1,0:T(1,128)}, f32[1,512]{1,0:T(1,128)}) custom-call(f32[16,120,128]{2,1,0:T(8,128)S(1)} %all_to_all.20.load_ref, f32[320,512]{1,0:T(8,128)S(1)} %copy-done.1, bf16[320,512]{1,0:T(8,128)(2,1)S(1)} %bitcast.15, f32[16,512]{1,0:T(8,128)S(1)} %copy-done.3, ...), custom_call_target="tpu_custom_call" | custom-call | tf_op jit(solution)/shard_map/final/pallas_call | solution.py:501
  (29 shorter events, 0.1 us)
Async XLA Ops:
  0.6 12.9 %collective-permute-start = (bf16[2,160,256]{2,1,0:T(8,128)(2,1)}, bf16[2,160,256]{2,1,0:T(8,128)(2,1)S(1)}, u32[]{:S(2)}, u32[]{:S(2)}) collective-permute-start(bf16[2,160,256]{2,1,0:T(8,128)(2,1)} %bitcast.22), channel_id=1, source_target_pairs={{4,0},{5,1},{6,2},{7,3},{8,4},{9,5},{10,6},{11,7},{12,8},{13,9},{1... | collective-permute-start | bytes 491528 | tf_op jit(solution)/shard_map/ppermute | solution.py:414
  2.9 20.8 %all-to-all-start = ((f32[16,8,128]{2,1,0:T(8,128)}), f32[16,8,128]{2,1,0:T(8,128)S(1)}, u32[]{:S(2)}, u32[]{:S(2)}) async-start(f32[16,8,128]{2,1,0:T(8,128)} %stats.1), calls=%async_computation | async-start | bytes 131072 | tf_op jit(solution)/shard_map/all_to_all | solution.py:406
  13.5 0.7 copy-start.7
  23.7 0.6 copy-start.8
  25.9 6.1 %copy-start.6 = (bf16[2,1,160,256]{3,2,1,0:T(8,128)(2,1)S(1)}, bf16[2,1,160,256]{3,2,1,0:T(8,128)(2,1)}, u32[]{:S(2)}) copy-start(bf16[2,1,160,256]{3,2,1,0:T(8,128)(2,1)} %param.9) | copy-start | bytes 491524
  26.0 47.8 %all-to-all-start.1 = ((bf16[16,448,128]{2,1,0:T(8,128)(2,1)}), bf16[16,448,128]{2,1,0:T(8,128)(2,1)}, u32[]{:S(2)}, u32[]{:S(2)}) async-start(bf16[16,448,128]{2,1,0:T(8,128)(2,1)} %combine.1), calls=%async_computation.1 | async-start | bytes 3670016 | tf_op jit(solution)/shard_map/all_to_all | solution.py:403
  32.1 29.2 %collective-permute-start.1 = (bf16[2,160,256]{2,1,0:T(8,128)(2,1)S(1)}, bf16[2,160,256]{2,1,0:T(8,128)(2,1)S(1)}, u32[]{:S(2)}, u32[]{:S(2)}) collective-permute-start(bf16[2,160,256]{2,1,0:T(8,128)(2,1)S(1)} %bitcast.25), channel_id=1, source_target_pairs={{3,0},{0,1},{1,2},{2,3},{7,4},{4,5},{5,6},{6,7},{11,8},{8,9},{9,10... | collective-permute-start | bytes 491528 | tf_op jit(solution)/shard_map/ppermute | solution.py:414
  33.6 27.6 %collective-permute-start.2 = (bf16[2,160,256]{2,1,0:T(8,128)(2,1)S(1)}, bf16[2,160,256]{2,1,0:T(8,128)(2,1)S(1)}, u32[]{:S(2)}, u32[]{:S(2)}) collective-permute-start(bf16[2,160,256]{2,1,0:T(8,128)(2,1)S(1)} %bitcast.26), channel_id=1, source_target_pairs={{1,0},{2,1},{3,2},{0,3},{5,4},{6,5},{7,6},{4,7},{9,8},{10,9},{11,1... | collective-permute-start | bytes 491528 | tf_op jit(solution)/shard_map/ppermute | solution.py:414
  35.4 27.2 %collective-permute-start.3 = (bf16[2,160,256]{2,1,0:T(8,128)(2,1)S(1)}, bf16[2,160,256]{2,1,0:T(8,128)(2,1)S(1)}, u32[]{:S(2)}, u32[]{:S(2)}) collective-permute-start(bf16[2,160,256]{2,1,0:T(8,128)(2,1)S(1)} %bitcast.27), channel_id=1, source_target_pairs={{7,0},{4,1},{5,2},{6,3},{11,4},{8,5},{9,6},{10,7},{15,8},{12,9},{1... | collective-permute-start | bytes 491528 | tf_op jit(solution)/shard_map/ppermute | solution.py:414
  35.4 27.2 %collective-permute-start.4 = (bf16[2,160,256]{2,1,0:T(8,128)(2,1)S(1)}, bf16[2,160,256]{2,1,0:T(8,128)(2,1)S(1)}, u32[]{:S(2)}, u32[]{:S(2)}) collective-permute-start(bf16[2,160,256]{2,1,0:T(8,128)(2,1)S(1)} %bitcast.28), channel_id=1, source_target_pairs={{5,0},{6,1},{7,2},{4,3},{9,4},{10,5},{11,6},{8,7},{13,8},{14,9},{1... | collective-permute-start | bytes 491528 | tf_op jit(solution)/shard_map/ppermute | solution.py:414
  61.2 1.4 %copy-start.9 = (bf16[2,160,256]{2,1,0:T(8,128)(2,1)}, bf16[2,160,256]{2,1,0:T(8,128)(2,1)S(1)}, u32[]{:S(2)}) copy-start(bf16[2,160,256]{2,1,0:T(8,128)(2,1)S(1)} %collective-permute-done.1.above_ref) | copy-start | bytes 491524
  61.2 1.4 %copy-start.10 = (bf16[2,160,256]{2,1,0:T(8,128)(2,1)}, bf16[2,160,256]{2,1,0:T(8,128)(2,1)S(1)}, u32[]{:S(2)}) copy-start(bf16[2,160,256]{2,1,0:T(8,128)(2,1)S(1)} %collective-permute-done.2.below_ref) | copy-start | bytes 491524
  62.6 0.7 copy-start.11
  63.3 0.7 copy-start.12
  73.7 8.8 %copy-start.4 = (f32[512]{0:T(512)S(1)}, f32[512]{0:T(512)}, u32[]{:S(2)}) copy-start(f32[512]{0:T(512)} %param.6) | copy-start | bytes 6148
  73.7 8.8 %copy-start.5 = (f32[512]{0:T(512)S(1)}, f32[512]{0:T(512)}, u32[]{:S(2)}) copy-start(f32[512]{0:T(512)} %param.7) | copy-start | bytes 6148
  77.3 5.2 %collective-permute-start.5 = (bf16[4,4,112,128]{3,2,1,0:T(8,128)(2,1)}, bf16[4,4,112,128]{3,2,1,0:T(8,128)(2,1)S(1)}, u32[]{:S(2)}, u32[]{:S(2)}) collective-permute-start(bf16[4,4,112,128]{3,2,1,0:T(8,128)(2,1)} %get-tuple-element.12), channel_id=1, source_target_pairs={{0,4},{4,0},{8,12},{12,8},{16,20},{20,16},{24,28},{28,24},{32,36},... | collective-permute-start | bytes 1376264 | tf_op jit(solution)/shard_map/ppermute | solution.py:474
  77.3 11.4 %all-to-all-start.2 = ((f32[16,8,128]{2,1,0:T(8,128)}), f32[16,8,128]{2,1,0:T(8,128)S(1)}, u32[]{:S(2)}, u32[]{:S(2)}) async-start(f32[16,8,128]{2,1,0:T(8,128)} %get-tuple-element.14), calls=%async_computation.2 | async-start | bytes 131072 | tf_op jit(solution)/shard_map/all_to_all | solution.py:403
  82.5 0.8 copy-start.2
  88.7 31.3 %copy-start = (bf16[2,1,160,512]{3,2,1,0:T(8,128)(2,1)S(1)}, bf16[2,1,160,512]{3,2,1,0:T(8,128)(2,1)}, u32[]{:S(2)}) copy-start(bf16[2,1,160,512]{3,2,1,0:T(8,128)(2,1)} %param.5) | copy-start | bytes 983044
  88.7 31.3 %copy-start.1 = (f32[320,512]{1,0:T(8,128)S(1)}, f32[320,512]{1,0:T(8,128)}, u32[]{:S(2)}) copy-start(f32[320,512]{1,0:T(8,128)} %get-tuple-element.15.act_ref) | copy-start | bytes 1966084
  88.7 31.3 %copy-start.3 = (f32[16,512]{1,0:T(8,128)S(1)}, f32[16,512]{1,0:T(8,128)}, u32[]{:S(2)}) copy-start(f32[16,512]{1,0:T(8,128)} %get-tuple-element.13.norm_ref) | copy-start | bytes 98308
where the time goes:
time: 122 us; the launch traced here: 121 us
  waiting for transfers between devices  31.2 us (26%)
  blocking collectives  31.2 us (26%)
  starting transfers between devices  27.8 us (23%)
  Pallas kernels  27 us (22%)
  local copies, waits for them, and re-layouts  3.41 us (3%)
    all_to_all x1, blocking collectives, in_ranks(): lax.all_to_all(value, 'tm', 0, 0, tiled=True, axis_index_groups=ranks)  31.2 us
    ppermute x5, waiting for transfers between devices, neighbour(): return lax.ppermute(ups, ('tm', 'rows'), pairs)  24.7 us
    all_to_all x2, starting transfers between devices, in_teams(): lax.all_to_all(value, ('tm', 'rows'), 0, 0, tiled=True, axis_index_groups...  11.3 us
    all_to_all x1, starting transfers between devices, in_ranks(): lax.all_to_all(value, 'tm', 0, 0, tiled=True, axis_index_groups=ranks)  10.6 us
    pallas_call x1, Pallas kernels, on_device(): dense_call(ups, halos[1], halos[2], halos[0], halos[3], halos[4], weight)  9.79 us
    all_to_all x1, waiting for transfers between devices, in_ranks(): lax.all_to_all(value, 'tm', 0, 0, tiled=True, axis_index_groups=ranks)  6.5 us
    ppermute x5, starting transfers between devices, neighbour(): return lax.ppermute(ups, ('tm', 'rows'), pairs)  5.94 us
    pallas_call x1, Pallas kernels, on_device(): part = weight_call(load, other, norm, gain, bias)  5.42 us
  transfers between devices with their start and end apart: 9, of which 3 were waited for; matrix products, arithmetic and copies ran while one was open for 0% of the time, Pallas kernels for 17%

commit v1 on v0

--- a/solution.py
+++ b/solution.py
@@ -62,7 +62,7 @@
     return ahead, slab, behind
 
 
-def pack_kernel(teams, feats_ref, up_ref, later_ref, load_ref):
+def pack_kernel(teams, count, feats_ref, up_ref, later_ref, stats_ref, load_ref):
     positions, chans = feats_ref.shape
     cols = up_ref.shape[1]
     rows = load_ref.shape[1]
@@ -95,6 +95,10 @@
                     core = j % 2
                     part = share[core * size : (core + 1) * size]
                     load_ref[j, r, positions : positions + size, :] = part
+    parts = joined_stats(count, stats_ref)
+    for j in range(TEAM):
+        for r in range(rows):
+            load_ref[j, r, positions + HALF :, :] = parts
 
 
 def stats_kernel(feats_ref, out_ref):
@@ -109,7 +113,7 @@
     out_ref[...] = jnp.broadcast_to((mean + exact_dot(squares, second))[None], out_ref.shape)
 
 
-def combine_kernel(count, load_ref, stats_ref, out_ref, parts, sem):
+def joined_stats(count, stats_ref):
     stats = [stats_ref[g] for g in range(stats_ref.shape[0])]
     total = stats[0]
     for stat in stats[1:]:
@@ -124,12 +128,8 @@
     mid = (stat - high).astype(BF16).astype(F32)
     low = stat - high - mid
     row = iota((8, 128), 0)
-    rows = jnp.where(row == 0, high, jnp.where(row == 1, mid, jnp.where(row == 2, low, 0.0)))
-    rows = jnp.concatenate([rows, jnp.zeros_like(rows)], axis=0).astype(BF16)
-    parts[...] = jnp.broadcast_to(rows[None], parts.shape)
-    copy = pltpu.make_async_copy(parts, out_ref.at[:, pl.ds(out_ref.shape[1] - 16, 16)], sem)
-    copy.start()
-    copy.wait()
+    parts = jnp.where(row == 0, high, jnp.where(row == 1, mid, jnp.where(row == 2, low, 0.0)))
+    return jnp.concatenate([parts, jnp.zeros_like(parts)], axis=0).astype(BF16)
 
 
 def dense_kernel(
@@ -385,7 +385,6 @@
     wide = chans // TEAM
     count = positions * devices * (chans // GROUPS)
     vmem = pl.BlockSpec(memory_space=pltpu.VMEM)
-    far = pl.BlockSpec(memory_space=pltpu.HBM)
 
     def params(mebibytes):
         return pltpu.CompilerParams(vmem_limit_bytes=mebibytes * 1024 * 1024)
@@ -423,23 +422,14 @@
     )(feats)
     stats = in_ranks(stats)
     pack_call = pl.pallas_call(
-        functools.partial(pack_kernel, tms),
+        functools.partial(pack_kernel, tms, float(positions * (chans // GROUPS))),
+        in_specs=[pl.BlockSpec()] * 3 + [vmem],
         out_shape=jax.ShapeDtypeStruct((TEAM, rows, length, wide), BF16),
         compiler_params=params(62),
         name="pack",
     )
-    load = pack_call(feats, ups, halos[0])
-    load = pl.pallas_call(
-        functools.partial(combine_kernel, float(positions * (chans // GROUPS))),
-        in_specs=[far, vmem],
-        out_specs=far,
-        out_shape=jax.ShapeDtypeStruct((size, length, wide), BF16),
-        scratch_shapes=[pltpu.VMEM((size, 16, wide), BF16), pltpu.SemaphoreType.DMA],
-        input_output_aliases={0: 0},
-        compiler_params=params(61),
-        name="combine",
-    )(load.reshape(size, length, wide), stats)
-    load = in_teams(load).reshape(TEAM, rows, length, wide)
+    load = pack_call(feats, ups, halos[0], stats)
+    load = in_teams(load.reshape(size, length, wide)).reshape(TEAM, rows, length, wide)
 
     def whole(shape):
         return pl.BlockSpec(shape, lambda *s: (0,) * len(shape))

time: 122 us -> 124 us (1.016)
  blocking collectives: 31.2 us -> 52.1 us
  starting transfers between devices: 27.8 us -> 17.2 us
  waiting for transfers between devices: 31.2 us -> 24.7 us
  Pallas kernels: 27 us -> 25.5 us
    all_to_all x1 -> x2, blocking collectives: 31.2 us -> 52.1 us  [in_ranks(): lax.all_to_all(value, 'tm', 0, 0, tiled=True, axis_index_groups=ranks)]
    all_to_all x1 -> x0, starting transfers between devices: 10.6 us -> none  [in_ranks(): lax.all_to_all(value, 'tm', 0, 0, tiled=True, axis_index_groups=ranks)]
    all_to_all x1 -> x0, waiting for transfers between devices: 6.5 us -> none  [in_ranks(): lax.all_to_all(value, 'tm', 0, 0, tiled=True, axis_index_groups=ranks)]
    pallas_call x2 -> x1, Pallas kernels: 4.64 us -> 3.15 us  [on_device(): load = pack_call(feats, ups, halos[0], stats)]
    unnamed x26 -> x24, local copies, waits for them, and re-layouts: 3.41 us -> 2.77 us
  transfers between devices with their start and end apart: 9 -> 8, of which waited for: 3 -> 2; matrix products, arithmetic and copies ran while one was open for 0% -> 0% of each run, Pallas kernels for 17% -> 14%
where the time goes in v1:
time: 124 us; the launch traced here: 123 us
  blocking collectives  52.1 us (42%)
  Pallas kernels  25.5 us (21%)
  waiting for transfers between devices  24.7 us (20%)
  starting transfers between devices  17.2 us (14%)
  local copies, waits for them, and re-layouts  2.77 us (2%)
    all_to_all x2, blocking collectives, in_ranks(): lax.all_to_all(value, 'tm', 0, 0, tiled=True, axis_index_groups=ranks)  52.1 us
    ppermute x5, waiting for transfers between devices, neighbour(): return lax.ppermute(ups, ('tm', 'rows'), pairs)  24.7 us
    all_to_all x2, starting transfers between devices, in_teams(): lax.all_to_all(value, ('tm', 'rows'), 0, 0, tiled=True, axis_index_groups...  11.3 us
    pallas_call x1, Pallas kernels, on_device(): dense_call(ups, halos[1], halos[2], halos[0], halos[3], halos[4], weight)  9.8 us
    ppermute x5, starting transfers between devices, neighbour(): return lax.ppermute(ups, ('tm', 'rows'), pairs)  5.94 us
    pallas_call x1, Pallas kernels, on_device(): part = weight_call(load, other, norm, gain, bias)  5.43 us
    pallas_call x1, Pallas kernels, on_device(): pl.pallas_call(functools.partial(act_kernel, positions * groups), in_spec...  3.55 us
    pallas_call x1, Pallas kernels, on_device(): load = pack_call(feats, ups, halos[0], stats)  3.15 us
  transfers between devices with their start and end apart: 8, of which 2 were waited for; matrix products, arithmetic and copies ran while one was open for 0% of the time, Pallas kernels for 14%

profile of v1, /device:TPU:32, one launch (start us, length us, event | category | flops | bytes accessed | tf_op | source)
XLA Modules:
  0.0 123.1 jit_solution(877247416957603192)
XLA Ops:
  0.6 0.1 collective-permute-start
  0.7 2.2 %stats.1 = f32[16,8,128]{2,1,0:T(8,128)} custom-call(bf16[320,512]{1,0:T(8,128)(2,1)} %bitcast.12), custom_call_target="tpu_custom_call" | custom-call | tf_op jit(solution)/shard_map/stats/pallas_call | solution.py:417
  2.9 20.9 %all_to_all.20.stats_ref = f32[16,8,128]{2,1,0:T(8,128)} all-to-all(f32[16,8,128]{2,1,0:T(8,128)} %stats.1), channel_id=1, replica_groups={{0,16,32,48,64,80,96,112,128,144,160,176,192,208,224,240},{4,20,36,52,6..., dimensions={0} | all-to-all | bytes 131072 | tf_op jit(solution)/shard_map/all_to_all | solution.py:405
  23.8 0.7 copy-done.7
  24.5 3.1 %pack.1 = bf16[4,4,448,128]{3,2,1,0:T(8,128)(2,1)} custom-call(bf16[320,512]{1,0:T(8,128)(2,1)} %bitcast.13, bf16[2,160,256]{2,1,0:T(8,128)(2,1)} %bitcast.23, bf16[2,160,256]{2,1,0:T(8,128)(2,1)} %copy-done.7, f32[16,8,128]{2,1,0:T(8,128)} %all_to_all.20.stats_ref), custom_call_target="tpu_custom_call" | custom-call | tf_op jit(solution)/shard_map/pack/pallas_call | solution.py:431
  27.6 6.1 %all-to-all-start.1 = ((bf16[16,448,128]{2,1,0:T(8,128)(2,1)}), bf16[16,448,128]{2,1,0:T(8,128)(2,1)}, u32[]{:S(2)}, u32[]{:S(2)}) async-start(bf16[16,448,128]{2,1,0:T(8,128)(2,1)} %bitcast.21), calls=%async_computation.1 | async-start | bytes 3670016 | tf_op jit(solution)/shard_map/all_to_all | solution.py:402
  33.7 1.5 %collective-permute-start.1 = (bf16[2,160,256]{2,1,0:T(8,128)(2,1)S(1)}, bf16[2,160,256]{2,1,0:T(8,128)(2,1)S(1)}, u32[]{:S(2)}, u32[]{:S(2)}) collective-permute-start(bf16[2,160,256]{2,1,0:T(8,128)(2,1)S(1)} %bitcast.25), channel_id=1, source_target_pairs={{3,0},{0,1},{1,2},{2,3},{7,4},{4,5},{5,6},{6,7},{11,8},{8,9},{9,10... | collective-permute-start | bytes 491528 | tf_op jit(solution)/shard_map/ppermute | solution.py:413
  35.3 1.8 %collective-permute-start.2 = (bf16[2,160,256]{2,1,0:T(8,128)(2,1)S(1)}, bf16[2,160,256]{2,1,0:T(8,128)(2,1)S(1)}, u32[]{:S(2)}, u32[]{:S(2)}) collective-permute-start(bf16[2,160,256]{2,1,0:T(8,128)(2,1)S(1)} %bitcast.26), channel_id=1, source_target_pairs={{1,0},{2,1},{3,2},{0,3},{5,4},{6,5},{7,6},{4,7},{9,8},{10,9},{11,1... | collective-permute-start | bytes 491528 | tf_op jit(solution)/shard_map/ppermute | solution.py:413
  37.0 0.0 collective-permute-start.3
  37.0 2.5 %collective-permute-start.4 = (bf16[2,160,256]{2,1,0:T(8,128)(2,1)S(1)}, bf16[2,160,256]{2,1,0:T(8,128)(2,1)S(1)}, u32[]{:S(2)}, u32[]{:S(2)}) collective-permute-start(bf16[2,160,256]{2,1,0:T(8,128)(2,1)S(1)} %bitcast.28), channel_id=1, source_target_pairs={{5,0},{6,1},{7,2},{4,3},{9,4},{10,5},{11,6},{8,7},{13,8},{14,9},{1... | collective-permute-start | bytes 491528 | tf_op jit(solution)/shard_map/ppermute | solution.py:413
  39.6 23.3 %collective-permute-done.1.above_ref = bf16[2,160,256]{2,1,0:T(8,128)(2,1)S(1)} collective-permute-done((bf16[2,160,256]{2,1,0:T(8,128)(2,1)S(1)}, bf16[2,160,256]{2,1,0:T(8,128)(2,1)S(1)}, u32[]{:S(2)}, u32[]{:S(2)}) %collective-permute-start.1) | collective-permute-done | bytes 163872 | tf_op jit(solution)/shard_map/ppermute | solution.py:413
  62.9 1.4 %collective-permute-done.3.later_above_ref = bf16[2,160,256]{2,1,0:T(8,128)(2,1)S(1)} collective-permute-done((bf16[2,160,256]{2,1,0:T(8,128)(2,1)S(1)}, bf16[2,160,256]{2,1,0:T(8,128)(2,1)S(1)}, u32[]{:S(2)}, u32[]{:S(2)}) %collective-permute-start.3) | collective-permute-done | bytes 163872 | tf_op jit(solution)/shard_map/ppermute | solution.py:413
  64.3 0.7 copy-done.10
  64.9 0.7 copy-done.11
  65.6 9.8 %dense.1.dense_ref = f32[320,512]{1,0:T(8,128)} custom-call(bf16[2,160,256]{2,1,0:T(8,128)(2,1)} %bitcast.24, bf16[2,160,256]{2,1,0:T(8,128)(2,1)} %copy-done.8, bf16[2,160,256]{2,1,0:T(8,128)(2,1)} %copy-done.9, bf16[2,160,256]{2,1,0:T(8,128)(2,1)} %copy-done.7, bf16[2,160,256]{2,1,0:T(8,128)(2,1)} %copy-done.10, bf16[2,160,256]{2,1,0:T(8,128)(2,1)} %copy-done.11, ...), custom_call_target="tpu_custom_call" | custom-call | tf_op jit(solution)/shard_map/dense/pallas_call | solution.py:450
  75.4 3.6 %act.1 = (f32[320,512]{1,0:T(8,128)}, f32[16,8,128]{2,1,0:T(8,128)}, f32[16,512]{1,0:T(8,128)}, bf16[4,4,112,128]{3,2,1,0:T(8,128)(2,1)}) custom-call(bf16[320,512]{1,0:T(8,128)(2,1)} %bitcast.14, f32[1,512]{1,0:T(1,128)} %bitcast.16, f32[1,512]{1,0:T(1,128)} %bitcast.19, bf16[4,4,448,128]{3,2,1,0:T(8,128)(2,1)} %bitcast.3.load_ref, f32[320,512]{1,0:T(8,128)} %dense.1.dense_ref), custom_call_target="tpu_custom_call" | custom-call | tf_op jit(solution)/shard_map/act/pallas_call | solution.py:452
  78.9 5.2 %all-to-all-start.2 = ((f32[16,8,128]{2,1,0:T(8,128)}), f32[16,8,128]{2,1,0:T(8,128)S(1)}, u32[]{:S(2)}, u32[]{:S(2)}) async-start(f32[16,8,128]{2,1,0:T(8,128)} %get-tuple-element.14), calls=%async_computation.2 | async-start | bytes 131072 | tf_op jit(solution)/shard_map/all_to_all | solution.py:402
  84.1 0.0 copy-start.2
  84.2 0.7 copy-done.2
  84.9 5.4 %wgrad.1.part_ref = f32[16,120,128]{2,1,0:T(8,128)S(1)} custom-call(bf16[4,4,448,128]{3,2,1,0:T(8,128)(2,1)} %bitcast.3.load_ref, bf16[4,4,112,128]{3,2,1,0:T(8,128)(2,1)S(1)} %collective-permute-done.5.other_ref, f32[16,512]{1,0:T(8,128)S(1)} %copy-done.2, f32[1,512]{1,0:T(1,128)S(1)} %bitcast.17, f32[1,512]{1,0:T(1,128)S(1)} %bitcast.20), custom_call_target="tpu_custom_call" | custom-call | tf_op jit(solution)/shard_map/wgrad/pallas_call | solution.py:479
  90.3 0.0 copy-start
  90.4 0.0 copy-start.3
  90.4 31.3 %all_to_all.21.load_ref = f32[16,120,128]{2,1,0:T(8,128)S(1)} all-to-all(f32[16,120,128]{2,1,0:T(8,128)S(1)} %append.1), channel_id=1, replica_groups={{0,16,32,48,64,80,96,112,128,144,160,176,192,208,224,240},{4,20,36,52,6..., dimensions={0} | all-to-all | bytes 1966080 | tf_op jit(solution)/shard_map/all_to_all | solution.py:405
  121.7 1.4 %final.1 = (bf16[320,512]{1,0:T(8,128)(2,1)}, f32[9,3,8,64]{3,2,1,0:T(8,128)}, f32[1,512]{1,0:T(1,128)}, f32[1,512]{1,0:T(1,128)}) custom-call(f32[16,120,128]{2,1,0:T(8,128)S(1)} %all_to_all.21.load_ref, f32[320,512]{1,0:T(8,128)S(1)} %copy-done.1, bf16[320,512]{1,0:T(8,128)(2,1)S(1)} %bitcast.15, f32[16,512]{1,0:T(8,128)S(1)} %copy-done.3, ...), custom_call_target="tpu_custom_call" | custom-call | tf_op jit(solution)/shard_map/final/pallas_call | solution.py:491
  (25 shorter events, 0.1 us)
Async XLA Ops:
  0.6 23.2 %collective-permute-start = (bf16[2,160,256]{2,1,0:T(8,128)(2,1)}, bf16[2,160,256]{2,1,0:T(8,128)(2,1)S(1)}, u32[]{:S(2)}, u32[]{:S(2)}) collective-permute-start(bf16[2,160,256]{2,1,0:T(8,128)(2,1)} %bitcast.22), channel_id=1, source_target_pairs={{4,0},{5,1},{6,2},{7,3},{8,4},{9,5},{10,6},{11,7},{12,8},{13,9},{1... | collective-permute-start | bytes 491528 | tf_op jit(solution)/shard_map/ppermute | solution.py:413
  23.8 0.7 copy-start.7
  27.6 6.1 %copy-start.6 = (bf16[2,1,160,256]{3,2,1,0:T(8,128)(2,1)S(1)}, bf16[2,1,160,256]{3,2,1,0:T(8,128)(2,1)}, u32[]{:S(2)}) copy-start(bf16[2,1,160,256]{3,2,1,0:T(8,128)(2,1)} %param.9) | copy-start | bytes 491524
  27.6 47.8 %all-to-all-start.1 = ((bf16[16,448,128]{2,1,0:T(8,128)(2,1)}), bf16[16,448,128]{2,1,0:T(8,128)(2,1)}, u32[]{:S(2)}, u32[]{:S(2)}) async-start(bf16[16,448,128]{2,1,0:T(8,128)(2,1)} %bitcast.21), calls=%async_computation.1 | async-start | bytes 3670016 | tf_op jit(solution)/shard_map/all_to_all | solution.py:402
  33.7 29.2 %collective-permute-start.1 = (bf16[2,160,256]{2,1,0:T(8,128)(2,1)S(1)}, bf16[2,160,256]{2,1,0:T(8,128)(2,1)S(1)}, u32[]{:S(2)}, u32[]{:S(2)}) collective-permute-start(bf16[2,160,256]{2,1,0:T(8,128)(2,1)S(1)} %bitcast.25), channel_id=1, source_target_pairs={{3,0},{0,1},{1,2},{2,3},{7,4},{4,5},{5,6},{6,7},{11,8},{8,9},{9,10... | collective-permute-start | bytes 491528 | tf_op jit(solution)/shard_map/ppermute | solution.py:413
  35.3 27.6 %collective-permute-start.2 = (bf16[2,160,256]{2,1,0:T(8,128)(2,1)S(1)}, bf16[2,160,256]{2,1,0:T(8,128)(2,1)S(1)}, u32[]{:S(2)}, u32[]{:S(2)}) collective-permute-start(bf16[2,160,256]{2,1,0:T(8,128)(2,1)S(1)} %bitcast.26), channel_id=1, source_target_pairs={{1,0},{2,1},{3,2},{0,3},{5,4},{6,5},{7,6},{4,7},{9,8},{10,9},{11,1... | collective-permute-start | bytes 491528 | tf_op jit(solution)/shard_map/ppermute | solution.py:413
  37.0 27.2 %collective-permute-start.3 = (bf16[2,160,256]{2,1,0:T(8,128)(2,1)S(1)}, bf16[2,160,256]{2,1,0:T(8,128)(2,1)S(1)}, u32[]{:S(2)}, u32[]{:S(2)}) collective-permute-start(bf16[2,160,256]{2,1,0:T(8,128)(2,1)S(1)} %bitcast.27), channel_id=1, source_target_pairs={{7,0},{4,1},{5,2},{6,3},{11,4},{8,5},{9,6},{10,7},{15,8},{12,9},{1... | collective-permute-start | bytes 491528 | tf_op jit(solution)/shard_map/ppermute | solution.py:413
  37.0 27.2 %collective-permute-start.4 = (bf16[2,160,256]{2,1,0:T(8,128)(2,1)S(1)}, bf16[2,160,256]{2,1,0:T(8,128)(2,1)S(1)}, u32[]{:S(2)}, u32[]{:S(2)}) collective-permute-start(bf16[2,160,256]{2,1,0:T(8,128)(2,1)S(1)} %bitcast.28), channel_id=1, source_target_pairs={{5,0},{6,1},{7,2},{4,3},{9,4},{10,5},{11,6},{8,7},{13,8},{14,9},{1... | collective-permute-start | bytes 491528 | tf_op jit(solution)/shard_map/ppermute | solution.py:413
  62.9 1.4 %copy-start.8 = (bf16[2,160,256]{2,1,0:T(8,128)(2,1)}, bf16[2,160,256]{2,1,0:T(8,128)(2,1)S(1)}, u32[]{:S(2)}) copy-start(bf16[2,160,256]{2,1,0:T(8,128)(2,1)S(1)} %collective-permute-done.1.above_ref) | copy-start | bytes 491524
  62.9 1.4 %copy-start.9 = (bf16[2,160,256]{2,1,0:T(8,128)(2,1)}, bf16[2,160,256]{2,1,0:T(8,128)(2,1)S(1)}, u32[]{:S(2)}) copy-start(bf16[2,160,256]{2,1,0:T(8,128)(2,1)S(1)} %collective-permute-done.2.below_ref) | copy-start | bytes 491524
  64.2 0.7 copy-start.10
  64.9 0.7 copy-start.11
  75.4 8.8 %copy-start.4 = (f32[512]{0:T(512)S(1)}, f32[512]{0:T(512)}, u32[]{:S(2)}) copy-start(f32[512]{0:T(512)} %param.6) | copy-start | bytes 6148
  75.4 8.8 %copy-start.5 = (f32[512]{0:T(512)S(1)}, f32[512]{0:T(512)}, u32[]{:S(2)}) copy-start(f32[512]{0:T(512)} %param.7) | copy-start | bytes 6148
  78.9 5.2 %collective-permute-start.5 = (bf16[4,4,112,128]{3,2,1,0:T(8,128)(2,1)}, bf16[4,4,112,128]{3,2,1,0:T(8,128)(2,1)S(1)}, u32[]{:S(2)}, u32[]{:S(2)}) collective-permute-start(bf16[4,4,112,128]{3,2,1,0:T(8,128)(2,1)} %get-tuple-element.12), channel_id=1, source_target_pairs={{0,4},{4,0},{8,12},{12,8},{16,20},{20,16},{24,28},{28,24},{32,36},... | collective-permute-start | bytes 1376264 | tf_op jit(solution)/shard_map/ppermute | solution.py:464
  78.9 11.4 %all-to-all-start.2 = ((f32[16,8,128]{2,1,0:T(8,128)}), f32[16,8,128]{2,1,0:T(8,128)S(1)}, u32[]{:S(2)}, u32[]{:S(2)}) async-start(f32[16,8,128]{2,1,0:T(8,128)} %get-tuple-element.14), calls=%async_computation.2 | async-start | bytes 131072 | tf_op jit(solution)/shard_map/all_to_all | solution.py:402
  84.1 0.8 copy-start.2
  90.3 31.3 %copy-start = (bf16[2,1,160,512]{3,2,1,0:T(8,128)(2,1)S(1)}, bf16[2,1,160,512]{3,2,1,0:T(8,128)(2,1)}, u32[]{:S(2)}) copy-start(bf16[2,1,160,512]{3,2,1,0:T(8,128)(2,1)} %param.5) | copy-start | bytes 983044
  90.3 31.3 %copy-start.1 = (f32[320,512]{1,0:T(8,128)S(1)}, f32[320,512]{1,0:T(8,128)}, u32[]{:S(2)}) copy-start(f32[320,512]{1,0:T(8,128)} %get-tuple-element.15.act_ref) | copy-start | bytes 1966084
  90.4 31.3 %copy-start.3 = (f32[16,512]{1,0:T(8,128)S(1)}, f32[16,512]{1,0:T(8,128)}, u32[]{:S(2)}) copy-start(f32[16,512]{1,0:T(8,128)} %get-tuple-element.13.norm_ref) | copy-start | bytes 98308

commit v2 on v1

--- a/solution.py
+++ b/solution.py
@@ -181,7 +181,13 @@
             out_ref[0:cols, :] += product(slabs[c, 2 - row_tap, 0], c)
 
 
-def norm_rows(stats, chans, positions):
+def norm_rows(load_ref, chans, positions):
+    stats = []
+    for j in range(load_ref.shape[0]):
+        for r in range(load_ref.shape[1]):
+            parts = load_ref[j, r, load_ref.shape[2] - 16 :].astype(F32)
+            stats.append(parts[0:1] + parts[1:2] + parts[2:3])
+    stats = jnp.concatenate(stats, axis=0)
     devices = stats.shape[0]
     size = chans // GROUPS
     first = members(chans, 0)
@@ -203,13 +209,8 @@
 ):
     chans = gain_ref.shape[1]
     start = load_ref.shape[2] - 16
-    stats = []
-    for j in range(load_ref.shape[0]):
-        for r in range(load_ref.shape[1]):
-            parts = load_ref[j, r, start:].astype(F32)
-            stats.append(parts[0:1] + parts[1:2] + parts[2:3])
     swap_ref[...] = load_ref[:, :, start - HALF : start, :]
-    centre, inverse = norm_rows(jnp.concatenate(stats, axis=0), chans, positions)
+    centre, inverse = norm_rows(load_ref, chans, positions)
     norm_ref[0:8] = centre
     norm_ref[8:16] = inverse
     centre = centre[0:1]
@@ -235,7 +236,7 @@
     out_ref[:, out_ref.shape[1] - total.shape[0] :, :] = jnp.broadcast_to(total[None], place)
 
 
-def weight_kernel(teams, load_ref, other_ref, norm_ref, gain_ref, bias_ref, out_ref, hidden, acc):
+def weight_kernel(teams, positions, load_ref, other_ref, gain_ref, bias_ref, out_ref, hidden, acc):
     time_index = lax.axis_index("tm")
     rows = load_ref.shape[1]
     cols = hidden.shape[2]
@@ -249,8 +250,7 @@
     def slice_of(value):
         return exact_dot(value, mover)[0:1]
 
-    centre = slice_of(norm_ref[0:8])
-    inverse = slice_of(norm_ref[8:16])
+    centre, inverse = (slice_of(value) for value in norm_rows(load_ref, chans, positions))
     gain = slice_of(jnp.broadcast_to(gain_ref[...], (8, chans)))
     bias = slice_of(jnp.broadcast_to(bias_ref[...], (8, chans)))
 
@@ -465,8 +465,8 @@
     sums = in_teams(sums)
 
     weight_call = pl.pallas_call(
-        functools.partial(weight_kernel, tms),
-        in_specs=[vmem] + [pl.BlockSpec()] * 4,
+        functools.partial(weight_kernel, tms, positions * groups),
+        in_specs=[vmem] + [pl.BlockSpec()] * 3,
         out_specs=vmem,
         out_shape=jax.ShapeDtypeStruct((groups, 14 * step + 8, 128), F32),
         scratch_shapes=[
@@ -476,7 +476,7 @@
         compiler_params=params(52),
         name="wgrad",
     )
-    part = weight_call(load, other, norm, gain, bias)
+    part = weight_call(load, other, gain, bias)
     part = pl.pallas_call(
         append_kernel,
         in_specs=[vmem, vmem],

time: 124 us -> 123 us (level)
  the two profiles are of different devices: /device:TPU:32 before, /device:TPU:0 now
where the time goes in v2:
time: 123 us
  blocking collectives  47 us (38%)
  Pallas kernels  27 us (22%)
  waiting for transfers between devices  24 us (20%)
  starting transfers between devices  21.9 us (18%)
  local copies, waits for them, and re-layouts  2.04 us (2%)
    all_to_all x2, blocking collectives, in_ranks(): lax.all_to_all(value, 'tm', 0, 0, tiled=True, axis_index_groups=ranks)  47 us
    ppermute x5, waiting for transfers between devices, neighbour(): return lax.ppermute(ups, ('tm', 'rows'), pairs)  23.7 us
    ppermute x5, starting transfers between devices, neighbour(): return lax.ppermute(ups, ('tm', 'rows'), pairs)  13.1 us
    pallas_call x1, Pallas kernels, on_device(): dense_call(ups, halos[1], halos[2], halos[0], halos[3], halos[4], weight)  11.1 us
    all_to_all x2, starting transfers between devices, in_teams(): lax.all_to_all(value, ('tm', 'rows'), 0, 0, tiled=True, axis_index_groups...  8.84 us
    pallas_call x1, Pallas kernels, on_device(): part = weight_call(load, other, gain, bias)  5.59 us
    pallas_call x1, Pallas kernels, on_device(): pl.pallas_call(functools.partial(act_kernel, positions * groups), in_spec...  3.57 us
    pallas_call x1, Pallas kernels, on_device(): load = pack_call(feats, ups, halos[0], stats)  3.14 us
  transfers between devices with their start and end apart: 8, of which 3 were waited for; matrix products, arithmetic and copies ran while one was open for 0% of the time, Pallas kernels for 15%

profile of v2, /device:TPU:0, one launch (start us, length us, event | category | flops | bytes accessed | tf_op | source)
XLA Modules:
  0.0 122.7 jit_solution(2461676222230705424)
XLA Ops:
  0.6 5.9 %collective-permute-start = (bf16[2,160,256]{2,1,0:T(8,128)(2,1)}, bf16[2,160,256]{2,1,0:T(8,128)(2,1)S(1)}, u32[]{:S(2)}, u32[]{:S(2)}) collective-permute-start(bf16[2,160,256]{2,1,0:T(8,128)(2,1)} %bitcast.22), channel_id=1, source_target_pairs={{4,0},{5,1},{6,2},{7,3},{8,4},{9,5},{10,6},{11,7},{12,8},{13,9},{1... | collective-permute-start | bytes 491528 | tf_op jit(solution)/shard_map/ppermute | solution.py:413
  6.5 2.2 %stats.1 = f32[16,8,128]{2,1,0:T(8,128)} custom-call(bf16[320,512]{1,0:T(8,128)(2,1)} %bitcast.12), custom_call_target="tpu_custom_call" | custom-call | tf_op jit(solution)/shard_map/stats/pallas_call | solution.py:417
  8.7 14.4 %all_to_all.20.stats_ref = f32[16,8,128]{2,1,0:T(8,128)} all-to-all(f32[16,8,128]{2,1,0:T(8,128)} %stats.1), channel_id=1, replica_groups={{0,16,32,48,64,80,96,112,128,144,160,176,192,208,224,240},{4,20,36,52,6..., dimensions={0} | all-to-all | bytes 131072 | tf_op jit(solution)/shard_map/all_to_all | solution.py:405
  23.1 0.7 copy-done.6
  23.7 3.1 %pack.1 = bf16[4,4,448,128]{3,2,1,0:T(8,128)(2,1)} custom-call(bf16[320,512]{1,0:T(8,128)(2,1)} %bitcast.13, bf16[2,160,256]{2,1,0:T(8,128)(2,1)} %bitcast.23, bf16[2,160,256]{2,1,0:T(8,128)(2,1)} %copy-done.6, f32[16,8,128]{2,1,0:T(8,128)} %all_to_all.20.stats_ref), custom_call_target="tpu_custom_call" | custom-call | tf_op jit(solution)/shard_map/pack/pallas_call | solution.py:431
  26.9 5.2 %all-to-all-start.1 = ((bf16[16,448,128]{2,1,0:T(8,128)(2,1)}), bf16[16,448,128]{2,1,0:T(8,128)(2,1)}, u32[]{:S(2)}, u32[]{:S(2)}) async-start(bf16[16,448,128]{2,1,0:T(8,128)(2,1)} %bitcast.21), calls=%async_computation.1 | async-start | bytes 3670016 | tf_op jit(solution)/shard_map/all_to_all | solution.py:402
  32.0 2.0 %collective-permute-start.1 = (bf16[2,160,256]{2,1,0:T(8,128)(2,1)S(1)}, bf16[2,160,256]{2,1,0:T(8,128)(2,1)S(1)}, u32[]{:S(2)}, u32[]{:S(2)}) collective-permute-start(bf16[2,160,256]{2,1,0:T(8,128)(2,1)S(1)} %bitcast.25), channel_id=1, source_target_pairs={{3,0},{0,1},{1,2},{2,3},{7,4},{4,5},{5,6},{6,7},{11,8},{8,9},{9,10... | collective-permute-start | bytes 491528 | tf_op jit(solution)/shard_map/ppermute | solution.py:413
  34.0 1.4 %collective-permute-start.2 = (bf16[2,160,256]{2,1,0:T(8,128)(2,1)S(1)}, bf16[2,160,256]{2,1,0:T(8,128)(2,1)S(1)}, u32[]{:S(2)}, u32[]{:S(2)}) collective-permute-start(bf16[2,160,256]{2,1,0:T(8,128)(2,1)S(1)} %bitcast.26), channel_id=1, source_target_pairs={{1,0},{2,1},{3,2},{0,3},{5,4},{6,5},{7,6},{4,7},{9,8},{10,9},{11,1... | collective-permute-start | bytes 491528 | tf_op jit(solution)/shard_map/ppermute | solution.py:413
  35.4 0.4 collective-permute-start.3
  35.7 3.5 %collective-permute-start.4 = (bf16[2,160,256]{2,1,0:T(8,128)(2,1)S(1)}, bf16[2,160,256]{2,1,0:T(8,128)(2,1)S(1)}, u32[]{:S(2)}, u32[]{:S(2)}) collective-permute-start(bf16[2,160,256]{2,1,0:T(8,128)(2,1)S(1)} %bitcast.28), channel_id=1, source_target_pairs={{5,0},{6,1},{7,2},{4,3},{9,4},{10,5},{11,6},{8,7},{13,8},{14,9},{1... | collective-permute-start | bytes 491528 | tf_op jit(solution)/shard_map/ppermute | solution.py:413
  39.3 22.3 %collective-permute-done.1.above_ref = bf16[2,160,256]{2,1,0:T(8,128)(2,1)S(1)} collective-permute-done((bf16[2,160,256]{2,1,0:T(8,128)(2,1)S(1)}, bf16[2,160,256]{2,1,0:T(8,128)(2,1)S(1)}, u32[]{:S(2)}, u32[]{:S(2)}) %collective-permute-start.1) | collective-permute-done | bytes 163872 | tf_op jit(solution)/shard_map/ppermute | solution.py:413
  61.6 1.4 %collective-permute-done.3.later_above_ref = bf16[2,160,256]{2,1,0:T(8,128)(2,1)S(1)} collective-permute-done((bf16[2,160,256]{2,1,0:T(8,128)(2,1)S(1)}, bf16[2,160,256]{2,1,0:T(8,128)(2,1)S(1)}, u32[]{:S(2)}, u32[]{:S(2)}) %collective-permute-start.3) | collective-permute-done | bytes 163872 | tf_op jit(solution)/shard_map/ppermute | solution.py:413
  63.0 0.7 copy-done.9
  63.7 0.7 copy-done.10
  64.3 11.1 %dense.1.dense_ref = f32[320,512]{1,0:T(8,128)} custom-call(bf16[2,160,256]{2,1,0:T(8,128)(2,1)} %bitcast.24, bf16[2,160,256]{2,1,0:T(8,128)(2,1)} %copy-done.7, bf16[2,160,256]{2,1,0:T(8,128)(2,1)} %copy-done.8, bf16[2,160,256]{2,1,0:T(8,128)(2,1)} %copy-done.6, bf16[2,160,256]{2,1,0:T(8,128)(2,1)} %copy-done.9, bf16[2,160,256]{2,1,0:T(8,128)(2,1)} %copy-done.10, ...), custom_call_target="tpu_custom_call" | custom-call | tf_op jit(solution)/shard_map/dense/pallas_call | solution.py:450
  75.4 0.0 all-to-all-done.1
  75.4 3.6 %act.1 = (f32[320,512]{1,0:T(8,128)}, f32[16,8,128]{2,1,0:T(8,128)}, f32[16,512]{1,0:T(8,128)}, bf16[4,4,112,128]{3,2,1,0:T(8,128)(2,1)}) custom-call(bf16[320,512]{1,0:T(8,128)(2,1)} %bitcast.14, f32[1,512]{1,0:T(1,128)} %bitcast.16, f32[1,512]{1,0:T(1,128)} %bitcast.19, bf16[4,4,448,128]{3,2,1,0:T(8,128)(2,1)} %bitcast.3.load_ref, f32[320,512]{1,0:T(8,128)} %dense.1.dense_ref), custom_call_target="tpu_custom_call" | custom-call | tf_op jit(solution)/shard_map/act/pallas_call | solution.py:452
  79.0 3.7 %all-to-all-start.2 = ((f32[16,8,128]{2,1,0:T(8,128)}), f32[16,8,128]{2,1,0:T(8,128)S(1)}, u32[]{:S(2)}, u32[]{:S(2)}) async-start(f32[16,8,128]{2,1,0:T(8,128)} %get-tuple-element.13), calls=%async_computation.2 | async-start | bytes 131072 | tf_op jit(solution)/shard_map/all_to_all | solution.py:402
  82.7 5.6 %wgrad.1.part_ref = f32[16,120,128]{2,1,0:T(8,128)S(1)} custom-call(bf16[4,4,448,128]{3,2,1,0:T(8,128)(2,1)} %bitcast.3.load_ref, bf16[4,4,112,128]{3,2,1,0:T(8,128)(2,1)S(1)} %collective-permute-done.5.other_ref, f32[1,512]{1,0:T(1,128)S(1)} %bitcast.17, f32[1,512]{1,0:T(1,128)S(1)} %bitcast.20), custom_call_target="tpu_custom_call" | custom-call | tf_op jit(solution)/shard_map/wgrad/pallas_call | solution.py:479
  88.3 0.0 copy-start
  88.3 0.0 copy-start.2
  88.4 0.2 all-to-all-done.2.load_ref
  88.6 32.7 %all_to_all.21.load_ref = f32[16,120,128]{2,1,0:T(8,128)S(1)} all-to-all(f32[16,120,128]{2,1,0:T(8,128)S(1)} %append.1), channel_id=1, replica_groups={{0,16,32,48,64,80,96,112,128,144,160,176,192,208,224,240},{4,20,36,52,6..., dimensions={0} | all-to-all | bytes 1966080 | tf_op jit(solution)/shard_map/all_to_all | solution.py:405
  121.3 1.4 %final.1 = (bf16[320,512]{1,0:T(8,128)(2,1)}, f32[9,3,8,64]{3,2,1,0:T(8,128)}, f32[1,512]{1,0:T(1,128)}, f32[1,512]{1,0:T(1,128)}) custom-call(f32[16,120,128]{2,1,0:T(8,128)S(1)} %all_to_all.21.load_ref, f32[320,512]{1,0:T(8,128)S(1)} %copy-done.1, bf16[320,512]{1,0:T(8,128)(2,1)S(1)} %bitcast.15, f32[16,512]{1,0:T(8,128)S(1)} %copy-done.2, ...), custom_call_target="tpu_custom_call" | custom-call | tf_op jit(solution)/shard_map/final/pallas_call | solution.py:491
  (23 shorter events, 0.1 us)
Async XLA Ops:
  0.6 22.4 %collective-permute-start = (bf16[2,160,256]{2,1,0:T(8,128)(2,1)}, bf16[2,160,256]{2,1,0:T(8,128)(2,1)S(1)}, u32[]{:S(2)}, u32[]{:S(2)}) collective-permute-start(bf16[2,160,256]{2,1,0:T(8,128)(2,1)} %bitcast.22), channel_id=1, source_target_pairs={{4,0},{5,1},{6,2},{7,3},{8,4},{9,5},{10,6},{11,7},{12,8},{13,9},{1... | collective-permute-start | bytes 491528 | tf_op jit(solution)/shard_map/ppermute | solution.py:413
  23.1 0.7 copy-start.6
  26.9 5.2 %copy-start.5 = (bf16[2,1,160,256]{3,2,1,0:T(8,128)(2,1)S(1)}, bf16[2,1,160,256]{3,2,1,0:T(8,128)(2,1)}, u32[]{:S(2)}) copy-start(bf16[2,1,160,256]{3,2,1,0:T(8,128)(2,1)} %param.9) | copy-start | bytes 491524
  26.9 48.6 %all-to-all-start.1 = ((bf16[16,448,128]{2,1,0:T(8,128)(2,1)}), bf16[16,448,128]{2,1,0:T(8,128)(2,1)}, u32[]{:S(2)}, u32[]{:S(2)}) async-start(bf16[16,448,128]{2,1,0:T(8,128)(2,1)} %bitcast.21), calls=%async_computation.1 | async-start | bytes 3670016 | tf_op jit(solution)/shard_map/all_to_all | solution.py:402
  32.0 29.6 %collective-permute-start.1 = (bf16[2,160,256]{2,1,0:T(8,128)(2,1)S(1)}, bf16[2,160,256]{2,1,0:T(8,128)(2,1)S(1)}, u32[]{:S(2)}, u32[]{:S(2)}) collective-permute-start(bf16[2,160,256]{2,1,0:T(8,128)(2,1)S(1)} %bitcast.25), channel_id=1, source_target_pairs={{3,0},{0,1},{1,2},{2,3},{7,4},{4,5},{5,6},{6,7},{11,8},{8,9},{9,10... | collective-permute-start | bytes 491528 | tf_op jit(solution)/shard_map/ppermute | solution.py:413
  34.0 27.6 %collective-permute-start.2 = (bf16[2,160,256]{2,1,0:T(8,128)(2,1)S(1)}, bf16[2,160,256]{2,1,0:T(8,128)(2,1)S(1)}, u32[]{:S(2)}, u32[]{:S(2)}) collective-permute-start(bf16[2,160,256]{2,1,0:T(8,128)(2,1)S(1)} %bitcast.26), channel_id=1, source_target_pairs={{1,0},{2,1},{3,2},{0,3},{5,4},{6,5},{7,6},{4,7},{9,8},{10,9},{11,1... | collective-permute-start | bytes 491528 | tf_op jit(solution)/shard_map/ppermute | solution.py:413
  35.4 27.6 %collective-permute-start.3 = (bf16[2,160,256]{2,1,0:T(8,128)(2,1)S(1)}, bf16[2,160,256]{2,1,0:T(8,128)(2,1)S(1)}, u32[]{:S(2)}, u32[]{:S(2)}) collective-permute-start(bf16[2,160,256]{2,1,0:T(8,128)(2,1)S(1)} %bitcast.27), channel_id=1, source_target_pairs={{7,0},{4,1},{5,2},{6,3},{11,4},{8,5},{9,6},{10,7},{15,8},{12,9},{1... | collective-permute-start | bytes 491528 | tf_op jit(solution)/shard_map/ppermute | solution.py:413
  35.7 27.3 %collective-permute-start.4 = (bf16[2,160,256]{2,1,0:T(8,128)(2,1)S(1)}, bf16[2,160,256]{2,1,0:T(8,128)(2,1)S(1)}, u32[]{:S(2)}, u32[]{:S(2)}) collective-permute-start(bf16[2,160,256]{2,1,0:T(8,128)(2,1)S(1)} %bitcast.28), channel_id=1, source_target_pairs={{5,0},{6,1},{7,2},{4,3},{9,4},{10,5},{11,6},{8,7},{13,8},{14,9},{1... | collective-permute-start | bytes 491528 | tf_op jit(solution)/shard_map/ppermute | solution.py:413
  61.6 1.4 %copy-start.7 = (bf16[2,160,256]{2,1,0:T(8,128)(2,1)}, bf16[2,160,256]{2,1,0:T(8,128)(2,1)S(1)}, u32[]{:S(2)}) copy-start(bf16[2,160,256]{2,1,0:T(8,128)(2,1)S(1)} %collective-permute-done.1.above_ref) | copy-start | bytes 491524
  61.6 1.4 %copy-start.8 = (bf16[2,160,256]{2,1,0:T(8,128)(2,1)}, bf16[2,160,256]{2,1,0:T(8,128)(2,1)S(1)}, u32[]{:S(2)}) copy-start(bf16[2,160,256]{2,1,0:T(8,128)(2,1)S(1)} %collective-permute-done.2.below_ref) | copy-start | bytes 491524
  63.0 0.7 copy-start.9
  63.7 0.7 copy-start.10
  75.4 7.3 %copy-start.3 = (f32[512]{0:T(512)S(1)}, f32[512]{0:T(512)}, u32[]{:S(2)}) copy-start(f32[512]{0:T(512)} %param.6) | copy-start | bytes 6148
  75.4 7.3 %copy-start.4 = (f32[512]{0:T(512)S(1)}, f32[512]{0:T(512)}, u32[]{:S(2)}) copy-start(f32[512]{0:T(512)} %param.7) | copy-start | bytes 6148
  79.0 3.7 %collective-permute-start.5 = (bf16[4,4,112,128]{3,2,1,0:T(8,128)(2,1)}, bf16[4,4,112,128]{3,2,1,0:T(8,128)(2,1)S(1)}, u32[]{:S(2)}, u32[]{:S(2)}) collective-permute-start(bf16[4,4,112,128]{3,2,1,0:T(8,128)(2,1)} %get-tuple-element.12), channel_id=1, source_target_pairs={{0,4},{4,0},{8,12},{12,8},{16,20},{20,16},{24,28},{28,24},{32,36},... | collective-permute-start | bytes 1376264 | tf_op jit(solution)/shard_map/ppermute | solution.py:464
  79.0 9.6 %all-to-all-start.2 = ((f32[16,8,128]{2,1,0:T(8,128)}), f32[16,8,128]{2,1,0:T(8,128)S(1)}, u32[]{:S(2)}, u32[]{:S(2)}) async-start(f32[16,8,128]{2,1,0:T(8,128)} %get-tuple-element.13), calls=%async_computation.2 | async-start | bytes 131072 | tf_op jit(solution)/shard_map/all_to_all | solution.py:402
  88.3 33.0 %copy-start = (bf16[2,1,160,512]{3,2,1,0:T(8,128)(2,1)S(1)}, bf16[2,1,160,512]{3,2,1,0:T(8,128)(2,1)}, u32[]{:S(2)}) copy-start(bf16[2,1,160,512]{3,2,1,0:T(8,128)(2,1)} %param.5) | copy-start | bytes 983044
  88.3 33.0 %copy-start.1 = (f32[320,512]{1,0:T(8,128)S(1)}, f32[320,512]{1,0:T(8,128)}, u32[]{:S(2)}) copy-start(f32[320,512]{1,0:T(8,128)} %get-tuple-element.14.act_ref) | copy-start | bytes 1966084
  88.3 32.9 %copy-start.2 = (f32[16,512]{1,0:T(8,128)S(1)}, f32[16,512]{1,0:T(8,128)}, u32[]{:S(2)}) copy-start(f32[16,512]{1,0:T(8,128)} %get-tuple-element.15.norm_ref) | copy-start | bytes 98308
